TPU v7x, 256 devices: a whole 4x4x8 slice. The times are simulated.
256 devices in a mesh: dp: 4 (over x), expert: 64 (over z, y, core).
Axes of the slice: x: 4, y: 4, z: 8, core: 2. Of those that a mesh axis runs over, the one named last changes fastest.
Arguments:
- hidden_acts: bfloat16 [4, 64, 1024, 768], P('dp', 'expert'), may hold values from -6 to 6
- out_grads: bfloat16 [4, 64, 1024, 2048], P('dp', 'expert'), may hold values from -0.29882812 to 0.29882812
- row_counts: int32 [4, 64], P('dp', 'expert'), may hold values from 128 to 1024, as said below
- plan_now: int32 [4, 64], replicated, may hold values from 0 to 23, as said below
- plan_next: int32 [4, 64], replicated, may hold values from 0 to 23, as said below
- master: float32 [24, 768, 2048], P(None, 'expert', 'dp'), may hold values from -6 to 6
- moment_one: float32 [24, 768, 2048], P(None, 'expert', 'dp'), may hold values from -6 to 6
- moment_two: float32 [24, 768, 2048], P(None, 'expert', 'dp'), may hold values from 0.01 to 0.3
Outputs:
- master_new: float32 [24, 768, 2048], P(None, 'expert', 'dp')
- moment_one_new: float32 [24, 768, 2048], P(None, 'expert', 'dp')
- moment_two_new: float32 [24, 768, 2048], P(None, 'expert', 'dp')
- replica_weights: bfloat16 [4, 64, 768, 2048], P('dp', 'expert')
Inputs may be any that keep to these rules, and one draw needn't show every extreme that they name: `plan_now`: every expert is named by 1 to 16 devices, and some expert by exactly 16. `plan_next`: every expert is named by 1 to 16 devices, and some expert by exactly 16. `row_counts`: A multiple of 128; rows from it on are padding. Some device has all 1024 rows live.
All inputs are finite; a program needn't handle non-finite values.
Results may differ from a plain program's by a relative error of at most 0.005.
Values may be sent and summed in bfloat16 or wider, within the bound.
A program may use at most 64 MiB of HBM per device.

v0:
```python
import jax
import jax.numpy as jnp
from jax import lax
from jax.sharding import PartitionSpec as P

beta_one = 0.9
beta_two = 0.999
learn_rate = 0.1
epsilon = 1e-08
first_fix = 1.0 - beta_one**10
second_fix = 1.0 - beta_two**10


def per_device(
    hidden_acts, out_grads, row_counts, plan_now, plan_next, master, moment_one, moment_two
):
    ex_count = lax.axis_size("expert")
    dp_index = lax.axis_index("dp")
    experts = master.shape[0]
    piece_rows = master.shape[1]
    hidden = hidden_acts[0, 0]
    upstream = out_grads[0, 0]
    width = upstream.shape[1]
    row_index = jnp.arange(hidden.shape[0], dtype=jnp.int32)
    row_mask = (row_index < row_counts[0, 0]).astype(hidden.dtype)[:, None]
    partial_value = lax.dot_general(
        hidden * row_mask, upstream, (((0,), (0,)), ((), ())), preferred_element_type=jnp.float32
    ).astype(jnp.bfloat16)
    expert_ids = jnp.arange(experts, dtype=jnp.int32)
    pieces = lax.all_to_all(
        partial_value.reshape(ex_count, piece_rows, width),
        "expert",
        split_axis=0,
        concat_axis=0,
        tiled=True,
    )
    sender_ids = lax.dynamic_index_in_dim(plan_now, dp_index, 0, keepdims=False)
    onehot = (sender_ids[None, :] == expert_ids[:, None]).astype(jnp.bfloat16)
    totals = jnp.einsum("es,srd->erd", onehot, pieces, preferred_element_type=jnp.float32)
    grad_sum = lax.psum_scatter(
        totals.astype(jnp.bfloat16), "dp", scatter_dimension=2, tiled=True
    ).astype(jnp.float32)
    moment_one_new = beta_one * moment_one + (1.0 - beta_one) * grad_sum
    moment_two_new = beta_two * moment_two + (1.0 - beta_two) * grad_sum * grad_sum
    master_new = master - learn_rate * (moment_one_new / first_fix) / (
        jnp.sqrt(moment_two_new / second_fix) + epsilon
    )
    rounded = master_new.astype(jnp.bfloat16)
    full_cols = lax.all_gather(rounded, "dp", axis=2, tiled=True)
    targets = lax.dynamic_index_in_dim(plan_next, dp_index, 0, keepdims=False)
    outgoing = jnp.take(full_cols, targets, axis=0)
    incoming = lax.all_to_all(outgoing, "expert", split_axis=0, concat_axis=0, tiled=True)
    replica = incoming.reshape(ex_count * piece_rows, width)
    return (master_new, moment_one_new, moment_two_new, replica[None, None])


def solution(mesh):
    return jax.shard_map(
        per_device,
        mesh=mesh,
        in_specs=(
            P("dp", "expert", None, None),
            P("dp", "expert", None, None),
            P("dp", "expert"),
            P(),
            P(),
            P(None, "expert", "dp"),
            P(None, "expert", "dp"),
            P(None, "expert", "dp"),
        ),
        out_specs=(
            P(None, "expert", "dp"),
            P(None, "expert", "dp"),
            P(None, "expert", "dp"),
            P("dp", "expert", None, None),
        ),
        check_vma=False,
    )
```

profile of v0, /device:TPU:1, one launch (start us, length us, event | category | flops | bytes accessed | tf_op | source)
XLA Modules:
  0.0 310.7 jit_solution(10174371553919339833)
XLA Ops:
  7.2 0.0 copy-start
  7.9 6.2 %fusion.2 = bf16[768,2048]{1,0:T(8,128)(2,1)S(1)} fusion(bf16[1,1,1024,2048]{3,2,1,0:T(8,128)(2,1)} %param.9, bf16[1,1,1024,768]{3,2,1,0:T(8,128)(2,1)} %param.8, bf16[1024]{0:T(1024)(128)(2,1)S(1)} %fusion.18), kind=kOutput, calls=%fused_computation.4 | convolution fusion | flops 3223584768 | bytes 8914944 | tf_op jit(solution)/shard_map/dot_general | solution.py:26
  14.1 2.7 reshape.58
  16.8 13.3 %all-to-all-start = ((bf16[64,12,2048]{2,1,0:T(8,128)(2,1)}), bf16[64,12,2048]{2,1,0:T(8,128)(2,1)}, u32[]{:S(2)}, u32[]{:S(2)}) async-start(bf16[64,12,2048]{2,1,0:T(8,128)(2,1)} %reshape.58), calls=%async_computation | async-start | bytes 8388608 | tf_op jit(solution)/shard_map/all_to_all | solution.py:30
  30.2 0.0 copy-start.1
  30.2 0.0 copy-start.2
  30.2 0.0 copy-start.3
  30.2 0.0 reduce-scatter.2.cloned.1.call-start
  30.2 0.0 copy-done
  30.3 0.0 copy-start.4
  30.3 94.3 %all-to-all-done = bf16[64,12,2048]{2,1,0:T(8,128)(2,1)} async-done(((bf16[64,12,2048]{2,1,0:T(8,128)(2,1)}), bf16[64,12,2048]{2,1,0:T(8,128)(2,1)}, u32[]{:S(2)}, u32[]{:S(2)}) %all-to-all-start) | async-done | bytes 3145760 | tf_op jit(solution)/shard_map/all_to_all | solution.py:30
  124.6 6.6 %fusion.7 = bf16[24,12,2048]{2,0,1:T(8,128)(2,1)} fusion(bf16[64,12,2048]{2,1,0:T(8,128)(2,1)} %all-to-all-done, s32[64]{0:T(128)S(1)} %dynamic-slice_bitcast_fusion), kind=kOutput, calls=%fused_computation.7 | convolution fusion | flops 76088832 | bytes 4325632 | tf_op jit(solution)/shard_map/es,srd->erd/dot_general | solution.py:39
  131.2 0.0 reduce-scatter.2.cloned.1.call-update
  131.2 0.0 all-gather.2.cloned.1.call-start
  131.3 23.3 %reduce-scatter.2.cloned.1.call-done = bf16[24,12,512]{2,0,1:T(8,128)(2,1)} async-done(((bf16[24,12,2048]{2,0,1:T(8,128)(2,1)}), bf16[24,12,512]{2,0,1:T(8,128)(2,1)}) %reduce-scatter.2.cloned.1.call-update) | async-done | bytes 294928 | tf_op jit(solution)/shard_map/reduce_scatter | solution.py:40
  154.6 0.0 copy-done.1
  154.6 0.0 copy-done.2
  154.6 0.0 copy-done.3
  154.6 2.5 fusion.20
  157.1 0.0 all-gather.2.cloned.1.call-update
  157.1 0.0 copy-done.4
  157.2 27.0 %all-gather.2.cloned.1.call-done = bf16[24,12,2048]{2,0,1:T(8,128)(2,1)} async-done(((bf16[24,12,512]{2,0,1:T(8,128)(2,1)}), bf16[24,12,2048]{2,0,1:T(8,128)(2,1)}) %all-gather.2.cloned.1.call-update) | async-done | bytes 1179664 | tf_op jit(solution)/shard_map/all_gather | solution.py:49
  184.2 1.9 copy.16
  186.2 2.8 gather_fusion
  188.9 2.6 broadcast_select_fusion
  191.6 106.2 %all_to_all.10 = bf16[64,12,2048]{2,1,0:T(8,128)(2,1)} all-to-all(bf16[64,12,2048]{2,1,0:T(8,128)(2,1)S(1)} %broadcast_select_fusion), channel_id=1, replica_groups=mesh['dp'=4,'expert'=64] {'expert'}, dimensions={0} | all-to-all | bytes 6291456 | tf_op jit(solution)/shard_map/all_to_all | solution.py:52
  297.7 6.2 %broadcast_in_dim_reshape.3 = bf16[1,1,768,2048]{3,2,1,0:T(8,128)(2,1)} reshape(bf16[64,12,2048]{2,1,0:T(8,128)(2,1)} %all_to_all.10) | data formatting | bytes 6291456 | tf_op jit(solution)/shard_map/broadcast_in_dim;reshape | solution.py:54
  (5 shorter events, 0.0 us)
Async XLA Ops:
  7.2 23.1 %copy-start = (s32[4,64]{1,0:T(4,128)S(1)}, s32[4,64]{1,0:T(4,128)}, u32[]{:S(2)}) copy-start(s32[4,64]{1,0:T(4,128)} %param.11) | copy-start | bytes 3076
  16.8 107.8 %all-to-all-start = ((bf16[64,12,2048]{2,1,0:T(8,128)(2,1)}), bf16[64,12,2048]{2,1,0:T(8,128)(2,1)}, u32[]{:S(2)}, u32[]{:S(2)}) async-start(bf16[64,12,2048]{2,1,0:T(8,128)(2,1)} %reshape.58), calls=%async_computation | async-start | bytes 8388608 | tf_op jit(solution)/shard_map/all_to_all | solution.py:30
  30.2 124.4 %copy-start.1 = (f32[24,12,512]{2,0,1:T(8,128)S(1)}, f32[24,12,512]{2,0,1:T(8,128)}, u32[]{:S(2)}) copy-start(f32[24,12,512]{2,0,1:T(8,128)} %param.13) | copy-start | bytes 1769476
  30.2 124.4 %copy-start.2 = (f32[24,12,512]{2,0,1:T(8,128)S(1)}, f32[24,12,512]{2,0,1:T(8,128)}, u32[]{:S(2)}) copy-start(f32[24,12,512]{2,0,1:T(8,128)} %param.14) | copy-start | bytes 1769476
  30.2 124.4 %copy-start.3 = (f32[24,12,512]{2,0,1:T(8,128)S(1)}, f32[24,12,512]{2,0,1:T(8,128)}, u32[]{:S(2)}) copy-start(f32[24,12,512]{2,0,1:T(8,128)} %param.15) | copy-start | bytes 1769476
  30.2 124.4 %reduce-scatter.2.cloned.1.call-start = ((), (), s32[]{:S(2)}) async-start(), calls=%async_computation.3 | async-start | bytes 1474560 | tf_op jit(solution)/shard_map/reduce_scatter | solution.py:40
  30.3 126.9 %copy-start.4 = (s32[4,64]{1,0:T(4,128)S(1)}, s32[4,64]{1,0:T(4,128)}, u32[]{:S(2)}) copy-start(s32[4,64]{1,0:T(4,128)} %param.12) | copy-start | bytes 3076
  131.2 53.0 %all-gather.2.cloned.1.call-start = ((), (), s32[]{:S(2)}) async-start(), calls=%async_computation.4 | async-start | bytes 1474560 | tf_op jit(solution)/shard_map/all_gather | solution.py:49
Sparse Core Ops, SparseCore 0:
  131.4 23.1 reduce-scatter.1
  157.3 26.9 all-gather.1
where the time goes:
time: 312 us; the launch traced here: 311 us
  waiting for transfers between devices  145 us (46%)
  blocking collectives  106 us (34%)
  between operations  14.8 us (5%)
  local copies, waits for them, and re-layouts  13.6 us (4%)
  starting transfers between devices  13.4 us (4%)
  matrix products  12.9 us (4%)
  other arithmetic  5.2 us (2%)
    all_to_all x1, blocking collectives, per_device(): lax.all_to_all(outgoing, 'expert', split_axis=0, concat_axis=0, tiled=True)  106 us
    all_to_all x1, waiting for transfers between devices, per_device(): lax.all_to_all(partial_value.reshape(ex_count, piece_rows, width), 'exper...  94.3 us
    all_gather x1, waiting for transfers between devices, per_device(): full_cols = lax.all_gather(rounded, 'dp', axis=2, tiled=True)  27 us
    reduce_scatter x1, waiting for transfers between devices, per_device(): lax.psum_scatter(totals.astype(jnp.bfloat16), 'dp', scatter_dimension=2,...  23.3 us
    all_to_all x1, starting transfers between devices, per_device(): lax.all_to_all(partial_value.reshape(ex_count, piece_rows, width), 'exper...  13.3 us
    dot_general x1, matrix products, per_device(): jnp.einsum('es,srd->erd', onehot, pieces, preferred_element_type=jnp.floa...  6.64 us
  transfers between devices with their start and end apart: 3, of which 3 were waited for; matrix products, arithmetic and copies ran while one was open for 0% of the time, Pallas kernels for 0%

commit v1 on v0

v1 whole, which is shorter than its diff:
```python
import functools

import jax
import jax.numpy as jnp
from jax import lax
from jax.experimental import pallas as pl
from jax.experimental.pallas import tpu as pltpu
from jax.sharding import PartitionSpec as P

beta_one = 0.9
beta_two = 0.999
learn_rate = 0.1
epsilon = 1e-08
first_fix = 1.0 - beta_one**10
second_fix = 1.0 - beta_two**10

MESH = pl.DeviceIdType.MESH
BF16 = jnp.bfloat16
F32 = jnp.float32
EXPERTS = 24
PLANE = 32
OUT_GROUPS = ((0, 1), (1, 3), (3, 5), (5, 8))
IN_GROUPS = ((0, 1), (1, 3), (3, 5), (5, 7), (7, 8))


def place():
    o = lax.axis_index("expert")
    return lax.axis_index("dp"), o // 8, lax.rem(o // 2, 4), lax.rem(o, 2)


def device(x, z, y, c):
    return (x, z * 8 + y * 2 + c)


def peer(index):
    x, z, y, c = place()
    t = lax.rem(index, 4)
    dx = lax.rem(1 + 2 * t + t // 2, 4)
    dy = lax.rem(dx + 1 + lax.rem(index // 4, 4), 4)
    dc = 1 - index // 16
    return lax.rem(x + dx, 4), lax.rem(y + dy, 4), lax.rem(c + dc, 2)


def meet():
    x, z, y, c = place()
    barrier = pltpu.get_barrier_semaphore()

    @pl.loop(0, PLANE - 1)
    def _(index):
        px, py, pc = peer(index)
        pl.semaphore_signal(barrier, inc=1, device_id=device(px, z, py, pc), device_id_type=MESH)

    for step in (1, 7):
        pl.semaphore_signal(
            barrier, inc=1, device_id=device(x, lax.rem(z + step, 8), y, c), device_id_type=MESH
        )
    return barrier


def all_met(barrier):
    pl.semaphore_wait(barrier, PLANE + 1)


def remote(src, dst, send_sem, recv_sem, target):
    return pltpu.make_async_remote_copy(
        src_ref=src, dst_ref=dst, send_sem=send_sem, recv_sem=recv_sem, device_id=target, device_id_type=MESH
    )


def drain(ref, sem):
    pltpu.make_async_copy(ref, ref, sem).wait()


def reduce_kernel(
    count, prev, last, hid, grd, own,
    hid_t, part, pieces, acc, up_s, up_r, down_s, down_r, total, swap_s, swap_r,
    plane_send, plane_recv, self_sem, ring_send, ring_recv, swap_sem,
):
    x, z, y, c = place()
    slot = (x * 4 + y) * 2 + c
    barrier = meet()
    rows = hid.shape[0]
    live = lax.broadcasted_iota(jnp.int32, (256, 1), 0)

    for k in range(rows // 256):
        block = hid[k * 256 : (k + 1) * 256, :]
        kept = jnp.where(live + k * 256 < count[0, 0], block.astype(F32), 0.0)
        hid_t[:, k * 256 : (k + 1) * 256] = kept.T.astype(BF16)

    def multiply(half):
        for px in range(4):
            col = px * 512 + half * 128
            rhs = jnp.concatenate([grd[:, col : col + 128], grd[:, col + 256 : col + 384]], axis=1)
            out = jnp.dot(hid_t[...], rhs, preferred_element_type=F32)
            for dest in range(8):
                away = lax.rem(dest - z + 8, 8)
                pos = jnp.where(away == 0, 7, jnp.where(away < 4, 7 - 2 * away, 2 * (away - 4)))
                for py in range(4):
                    top = dest * 96 + py * 24
                    block = out[top : top + 24, :].astype(BF16)
                    part[pos, py, :, col : col + 128] = block[:, :128]
                    part[pos, py, :, col + 256 : col + 384] = block[:, 128:]

    def spread(half):
        for g, (a, b) in enumerate(OUT_GROUPS):

            @pl.loop(0, PLANE - 1)
            def _(index):
                px, py, pc = peer(index)
                col = pl.multiple_of(px * 512 + pc * 256 + half * 128, 128)
                remote(
                    part.at[a:b, py, :, pl.ds(col, 128)],
                    pieces.at[half, slot, a:b],
                    plane_send.at[half],
                    plane_recv.at[half, g],
                    device(px, z, py, pc),
                ).start()

        col = pl.multiple_of(x * 512 + c * 256 + half * 128, 128)
        pltpu.make_async_copy(
            part.at[:, y, :, pl.ds(col, 128)], pieces.at[half, slot], self_sem.at[half]
        ).start()

    def gather_up(half):
        zplus, zminus = lax.rem(z + 1, 8), lax.rem(z + 7, 8)
        acc[PLANE] = jnp.zeros_like(acc[PLANE])
        drain(pieces.at[half, 0], self_sem.at[half])
        for g, (a, b) in enumerate(OUT_GROUPS):
            drain(pieces.at[half, pl.ds(0, PLANE - 1), a:b], plane_recv.at[half, g])

            @pl.loop(0, PLANE)
            def _(i):
                acc[i, a:b] = pieces[half, i, a:b].astype(F32) + acc[prev[i], a:b]

            if g == 0:

                @pl.loop(0, EXPERTS // 2)
                def _(e):
                    up_s[half, 0, e] = acc[last[e], 0].astype(BF16)
                    down_s[half, 0, e] = acc[last[e + 12], 0].astype(BF16)

            else:
                for ring, (buf, r) in enumerate(((up_s, up_r), (down_s, down_r))):
                    first = half_of(ring) if g == 1 else slice(0, EXPERTS)
                    n = first.stop - first.start
                    drain(r.at[half, g - 1, pl.ds(0, n)], ring_recv.at[half, ring, g - 1])
                    pos = a + ring

                    @pl.loop(0, n)
                    def _(e):
                        buf[half, g, e + first.start] = (
                            acc[last[e + first.start], pos] + r[half, g - 1, e].astype(F32)
                        ).astype(BF16)

                    if g == 1:

                        @pl.loop(0, EXPERTS - n)
                        def _(e):
                            other = e + (12 - first.start)
                            buf[half, g, other] = acc[last[other], pos].astype(BF16)

            n = 12 if g == 0 else EXPERTS
            for ring, (s, r, to) in enumerate(((up_s, up_r, zplus), (down_s, down_r, zminus))):
                remote(
                    s.at[half, g, pl.ds(0, n)],
                    r.at[half, g, pl.ds(0, n)],
                    ring_send.at[half, ring, g],
                    ring_recv.at[half, ring, g],
                    device(x, to, y, c),
                ).start()

        for ring, r in enumerate((up_r, down_r)):
            drain(r.at[half, 3], ring_recv.at[half, ring, 3])

        @pl.loop(0, EXPERTS)
        def _(e):
            total[half, e] = acc[last[e], 7] + up_r[half, 3, e].astype(F32) + down_r[half, 3, e].astype(F32)

        col = pl.multiple_of(c * 256 + half * 128, 128)

        @pl.loop(0, EXPERTS)
        def _(e):
            low, high = total[half, e, 0:12, :], total[half, e, 12:24, :]
            own[e, :, pl.ds(col, 128)] = jnp.where(c == 0, low, high)
            swap_s[half, e] = jnp.where(c == 0, high, low)

        remote(
            swap_s.at[half], swap_r.at[half], swap_sem.at[half, 0], swap_sem.at[half, 1], device(x, z, y, 1 - c)
        ).start()

    multiply(0)
    all_met(barrier)
    spread(0)
    multiply(1)
    spread(1)
    gather_up(0)
    gather_up(1)
    for half in range(2):
        drain(swap_r.at[half], swap_sem.at[half, 1])
        col = pl.multiple_of((1 - c) * 256 + half * 128, 128)
        own[:, :, pl.ds(col, 128)] = swap_r[half]
    for half in range(2):
        drain(swap_s.at[half], swap_sem.at[half, 0])
        drain(pieces.at[half, pl.ds(0, PLANE - 1)], plane_send.at[half])
        for g in range(4):
            n = 12 if g == 0 else EXPERTS
            for ring, s in enumerate((up_s, down_s)):
                drain(s.at[half, g, pl.ds(0, n)], ring_send.at[half, ring, g])


def half_of(ring):
    return slice(12 * ring, 12 * ring + 12)


def expand_kernel(
    plan, new, out,
    swap_r, whole, held_00, held_01, held_02, held_03, held_04, held_10, held_11, held_12, held_13, held_14,
    picked, result,
    swap_sem, ring_send, ring_recv, plane_send, plane_recv, out_sem,
):
    held = ((held_00, held_01, held_02, held_03, held_04), (held_10, held_11, held_12, held_13, held_14))
    x, z, y, c = place()
    zplus, zminus = lax.rem(z + 1, 8), lax.rem(z + 7, 8)
    barrier = meet()
    all_met(barrier)
    for half in range(2):
        col = pl.multiple_of((1 - c) * 256 + half * 128, 128)
        remote(
            new.at[:, :, pl.ds(col, 128)],
            swap_r.at[half],
            swap_sem.at[half, 0],
            swap_sem.at[half, 1],
            device(x, z, y, 1 - c),
        ).start()
    for half in range(2):
        drain(swap_r.at[half], swap_sem.at[half, 1])
        col = pl.multiple_of(c * 256 + half * 128, 128)

        @pl.loop(0, EXPERTS)
        def _(e):
            mine, theirs = new[e, :, pl.ds(col, 128)], swap_r[half, e]
            whole[half, e, 0:12, :] = jnp.where(c == 0, mine, theirs)
            whole[half, e, 12:24, :] = jnp.where(c == 0, theirs, mine)

        held[half][0][0] = whole[half].astype(BF16)

    def hop(half, k):
        for ring, to in enumerate((zplus, zminus)):
            src = 0 if k == 0 else ring
            dst = 0 if k == 3 else ring
            part = pl.ds(12 * ring, 12) if k == 3 else pl.ds(0, EXPERTS)
            yield remote(
                held[half][k].at[src, part],
                held[half][k + 1].at[dst, part],
                ring_send.at[half, ring, k],
                ring_recv.at[half, ring, k],
                device(x, to, y, c),
            )

    for half in range(2):
        for copy in hop(half, 0):
            copy.start()
    for g, (a, b) in enumerate(IN_GROUPS):
        for half in range(2):
            if g:
                for copy in hop(half, g - 1):
                    copy.wait_recv()
                if g < 4:
                    for copy in hop(half, g):
                        copy.start()
            col = pl.multiple_of(x * 512 + c * 256 + half * 128, 128)

            @pl.loop(0, PLANE - 1)
            def _(index):
                px, py, pc = peer(index)
                e = plan[px, z * 8 + py * 2 + pc]
                picked[half, index, a:b] = held[half][g][:, e]
                remote(
                    picked.at[half, index, a:b],
                    result.at[a:b, y, :, pl.ds(col, 128)],
                    plane_send.at[half],
                    plane_recv.at[g],
                    device(px, z, py, pc),
                ).start()

            result[a:b, y, :, pl.ds(col, 128)] = held[half][g][:, plan[x, z * 8 + y * 2 + c]]
    for g, (a, b) in enumerate(IN_GROUPS):
        drain(picked.at[:, pl.ds(0, PLANE - 1), a:b], plane_recv.at[g])
        for pos in range(a, b):
            away = (0, 7, 1, 6, 2, 5, 3, 4)[pos]
            pltpu.make_async_copy(result.at[pos], out.at[lax.rem(z + away, 8)], out_sem.at[pos]).start()
    for pos in range(8):
        drain(result.at[pos], out_sem.at[pos])
    for half in range(2):
        drain(swap_r.at[half], swap_sem.at[half, 0])
        drain(picked.at[half, pl.ds(0, PLANE - 1)], plane_send.at[half])
        for k in range(4):
            for copy in hop(half, k):
                copy.wait_send()


VMEM = pl.BlockSpec(memory_space=pltpu.VMEM)
SMEM = pl.BlockSpec(memory_space=pltpu.SMEM)
ANY = pl.BlockSpec(memory_space=pl.ANY)
DMA = pltpu.SemaphoreType.DMA


def params(number):
    return pltpu.CompilerParams(collective_id=number, has_side_effects=True, vmem_limit_bytes=60 * 2**20)


def reduce_grads(count, prev, last, hidden, upstream):
    block = (24, 24, 128)
    return pl.pallas_call(
        reduce_kernel,
        out_shape=jax.ShapeDtypeStruct((24, 12, 512), F32),
        in_specs=[SMEM, SMEM, SMEM, VMEM, VMEM],
        out_specs=VMEM,
        scratch_shapes=[
            pltpu.VMEM((768, 1024), BF16),
            pltpu.VMEM((8, 4, 24, 2048), BF16),
            pltpu.VMEM((2, 32, 8, 24, 128), BF16),
            pltpu.VMEM((33, 8, 24, 128), F32),
        ]
        + [pltpu.VMEM((2, 4) + block, BF16)] * 4
        + [
            pltpu.VMEM((2,) + block, F32),
            pltpu.VMEM((2, 24, 12, 128), F32),
            pltpu.VMEM((2, 24, 12, 128), F32),
            DMA((2,)),
            DMA((2, 4)),
            DMA((2,)),
            DMA((2, 2, 4)),
            DMA((2, 2, 4)),
            DMA((2, 2)),
        ],
        compiler_params=params(0),
        name="reduce_grads",
    )(count, prev, last, hidden, upstream)


def expand_weights(plan_next, master_new):
    return pl.pallas_call(
        expand_kernel,
        out_shape=jax.ShapeDtypeStruct((8, 4, 24, 2048), BF16),
        in_specs=[SMEM, VMEM],
        out_specs=ANY,
        scratch_shapes=[
            pltpu.VMEM((2, 24, 12, 128), F32),
            pltpu.VMEM((2, 24, 24, 128), F32),
        ]
        + [pltpu.VMEM((b - a, 24, 24, 128), BF16) for _ in range(2) for a, b in IN_GROUPS]
        + [
            pltpu.VMEM((2, 31, 8, 24, 128), BF16),
            pltpu.VMEM((8, 4, 24, 2048), BF16),
            DMA((2, 2)),
            DMA((2, 2, 4)),
            DMA((2, 2, 4)),
            DMA((2,)),
            DMA((5,)),
            DMA((8,)),
        ],
        compiler_params=params(1),
        name="expand_weights",
    )(plan_next, master_new)


def per_device(hidden_acts, out_grads, row_counts, plan_now, plan_next, master, moment_one, moment_two):
    z = lax.axis_index("expert") // 8
    ids = lax.dynamic_slice_in_dim(plan_now, z * 8, 8, axis=1).reshape(PLANE)
    order = jnp.arange(PLANE, dtype=jnp.int32)
    earlier = (ids[None, :] == ids[:, None]) & (order[None, :] < order[:, None])
    prev = jnp.max(jnp.where(earlier, order[None, :], -1), axis=1)
    prev = jnp.where(prev < 0, PLANE, prev)
    named = ids[None, :] == jnp.arange(EXPERTS, dtype=jnp.int32)[:, None]
    last = jnp.max(jnp.where(named, order[None, :], -1), axis=1)
    last = jnp.where(last < 0, PLANE, last)
    grad_sum = reduce_grads(row_counts, prev, last, hidden_acts[0, 0], out_grads[0, 0])
    moment_one_new = beta_one * moment_one + (1.0 - beta_one) * grad_sum
    moment_two_new = beta_two * moment_two + (1.0 - beta_two) * grad_sum * grad_sum
    master_new = master - learn_rate * (moment_one_new / first_fix) / (
        jnp.sqrt(moment_two_new / second_fix) + epsilon
    )
    replica = expand_weights(plan_next, master_new)
    return (master_new, moment_one_new, moment_two_new, replica.reshape(1, 1, 768, 2048))


def solution(mesh):
    state = P(None, "expert", "dp")
    split = P("dp", "expert", None, None)
    return jax.shard_map(
        per_device,
        mesh=mesh,
        in_specs=(split, split, P("dp", "expert"), P(), P(), state, state, state),
        out_specs=(state, state, state, split),
        check_vma=False,
    )
```

time: 312 us -> 130 us (0.42)
  waiting for transfers between devices: 145 us -> 0 us
  Pallas kernels: 0 us -> 117 us
  blocking collectives: 106 us -> 0 us
  between operations: 14.8 us -> 1.36 us
  starting transfers between devices: 13.4 us -> 0 us
  matrix products: 12.9 us -> 0 us
  local copies, waits for them, and re-layouts: 13.6 us -> 7.64 us
    pallas_call x0 -> x2, Pallas kernels: none -> 117 us  [the longest x1 69.8 us: reduce_grads(): pl.pallas_call(reduce_kernel, out_shape=jax.ShapeDtypeStruct((24, 12, 512...]
    all_to_all x1 -> x0, blocking collectives: 106 us -> none  [per_device(): lax.all_to_all(outgoing, 'expert', split_axis=0, concat_axis=0, tiled=True)]
    all_to_all x1 -> x0, waiting for transfers between devices: 94.3 us -> none  [per_device(): lax.all_to_all(partial_value.reshape(ex_count, piece_rows, width), 'exper...]
    all_gather x1 -> x0, waiting for transfers between devices: 27 us -> none  [per_device(): full_cols = lax.all_gather(rounded, 'dp', axis=2, tiled=True)]
    reduce_scatter x1 -> x0, waiting for transfers between devices: 23.3 us -> none  [per_device(): lax.psum_scatter(totals.astype(jnp.bfloat16), 'dp', scatter_dimension=2,...]
    all_to_all x1 -> x0, starting transfers between devices: 13.3 us -> none  [per_device(): lax.all_to_all(partial_value.reshape(ex_count, piece_rows, width), 'exper...]
    dot_general x2 -> x0, matrix products: 12.9 us -> none  [the longest x1 6.64 us: per_device(): jnp.einsum('es,srd->erd', onehot, pieces, preferred_element_type=jnp.floa...]
    unnamed x10 -> x14, local copies, waits for them, and re-layouts: 0.03 us -> 7.48 us
  transfers between devices with their start and end apart: 3 -> 0, of which waited for: 3 -> 0; matrix products, arithmetic and copies ran while one was open for 0% -> 0% of each run, Pallas kernels for 0% -> 0%
where the time goes in v1:
time: 130 us
  Pallas kernels  117 us (90%)
  local copies, waits for them, and re-layouts  7.64 us (6%)
  other arithmetic  3.87 us (3%)
  between operations  1.36 us (1%)
    pallas_call x1, Pallas kernels, reduce_grads(): pl.pallas_call(reduce_kernel, out_shape=jax.ShapeDtypeStruct((24, 12, 512...  69.8 us
    pallas_call x1, Pallas kernels, expand_weights(): pl.pallas_call(expand_kernel, out_shape=jax.ShapeDtypeStruct((8, 4, 24, 2...  47 us
    unnamed x14, local copies, waits for them, and re-layouts  7.48 us

profile of v1, /device:TPU:1, one launch (start us, length us, event | category | flops | bytes accessed | tf_op | source)
XLA Modules:
  0.0 129.7 jit_solution(5510592150182317898)
XLA Ops:
  0.6 0.0 copy-start
  1.3 0.0 copy-done
  1.3 0.1 constant_dynamic-slice_fusion
  1.4 0.1 eq.28
  1.5 0.1 select_reduce_fusion.1
  1.6 0.2 select_reduce_fusion
  1.8 0.5 compare_select_fusion.1.prev
  2.3 0.5 compare_select_fusion.last
  2.8 0.0 copy-start.2
  2.8 0.0 copy-start.3
  2.8 0.0 copy-start.4
  2.8 69.8 %reduce_grads.1 = f32[24,12,512]{2,1,0:T(8,128)} custom-call(s32[1,1]{1,0:T(1,128)S(6)} %copy.34.count, s32[32]{0:T(128)} %compare_select_fusion.1.prev, s32[24]{0:T(128)} %compare_select_fusion.last, bf16[1024,768]{1,0:T(8,128)(2,1)} %bitcast.5, bf16[1024,2048]{1,0:T(8,128)(2,1)} %bitcast.4), custom_call_target="tpu_custom_call" | custom-call | tf_op jit(solution)/shard_map/reduce_grads/pallas_call | solution.py:314
  72.6 0.0 copy-done.2
  72.6 0.0 copy-done.3
  72.7 0.0 copy-done.4
  72.7 2.5 %copy_subtract_fusion = (f32[24,12,512]{2,1,0:T(8,128)S(1)}, f32[24,12,512]{2,1,0:T(8,128)S(1)}, f32[24,12,512]{2,1,0:T(8,128)S(1)}) fusion(f32[24,12,512]{2,0,1:T(8,128)S(1)} %copy-done.2, f32[24,12,512]{2,1,0:T(8,128)} %reduce_grads.1, f32[24,12,512]{2,0,1:T(8,128)S(1)} %copy-done.3, f32[24,12,512]{2,0,1:T(8,128)S(1)} %copy-done.4), kind=kLoop, calls=%fused_computation.2 | loop fusion | flops 1769472 | bytes 4128768 | tf_op jit(solution)/shard_map/sub | solution.py:381
  75.2 0.0 copy-start.1
  75.2 1.2 copy.22
  76.4 1.2 copy.23
  77.5 1.2 copy.21
  78.7 0.0 copy-done.1
  78.7 47.0 %expand_weights.1 = bf16[8,4,24,2048]{3,2,1,0:T(8,128)(2,1)} custom-call(s32[4,64]{1,0:T(4,128)} %plan.1, f32[24,12,512]{2,1,0:T(8,128)} %copy-done.1), custom_call_target="tpu_custom_call" | custom-call | tf_op jit(solution)/shard_map/expand_weights/pallas_call | solution.py:343
  125.7 4.0 %copy.35 = bf16[1,1,768,2048]{3,2,1,0:T(8,128)(2,1)} copy(bf16[1,1,768,2048]{3,2,1,0:T(8,128)(2,1)} %bitcast.3) | data formatting | bytes 6291456
Async XLA Ops:
  0.6 0.7 copy-start
  2.8 69.8 %copy-start.2 = (f32[24,12,512]{2,0,1:T(8,128)S(1)}, f32[24,12,512]{2,0,1:T(8,128)}, u32[]{:S(2)}) copy-start(f32[24,12,512]{2,0,1:T(8,128)} %param.13) | copy-start | bytes 1769476
  2.8 69.8 %copy-start.3 = (f32[24,12,512]{2,0,1:T(8,128)S(1)}, f32[24,12,512]{2,0,1:T(8,128)}, u32[]{:S(2)}) copy-start(f32[24,12,512]{2,0,1:T(8,128)} %param.14) | copy-start | bytes 1769476
  2.8 69.8 %copy-start.4 = (f32[24,12,512]{2,0,1:T(8,128)S(1)}, f32[24,12,512]{2,0,1:T(8,128)}, u32[]{:S(2)}) copy-start(f32[24,12,512]{2,0,1:T(8,128)} %param.15) | copy-start | bytes 1769476
  75.2 3.5 %copy-start.1 = (f32[24,12,512]{2,1,0:T(8,128)}, f32[24,12,512]{2,1,0:T(8,128)S(1)}, u32[]{:S(2)}) copy-start(f32[24,12,512]{2,1,0:T(8,128)S(1)} %get-tuple-element.12.new) | copy-start | bytes 1769476

commit v2 on v1

v2 whole, which is shorter than its diff:
```python
import functools

import jax
import jax.numpy as jnp
from jax import lax
from jax.experimental import pallas as pl
from jax.experimental.pallas import tpu as pltpu
from jax.sharding import PartitionSpec as P

beta_one = 0.9
beta_two = 0.999
learn_rate = 0.1
epsilon = 1e-08
first_fix = 1.0 - beta_one**10
second_fix = 1.0 - beta_two**10

MESH = pl.DeviceIdType.MESH
BF16 = jnp.bfloat16
F32 = jnp.float32
EXPERTS = 24
PLANE = 32
OUT_GROUPS = ((0, 1), (1, 3), (3, 5), (5, 8))
IN_GROUPS = ((0, 1), (1, 3), (3, 5), (5, 7), (7, 8))


def place():
    o = lax.axis_index("expert")
    return lax.axis_index("dp"), o // 8, lax.rem(o // 2, 4), lax.rem(o, 2)


def device(x, z, y, c):
    return (x, z * 8 + y * 2 + c)


def peer(index):
    x, z, y, c = place()
    t = lax.rem(index, 4)
    dx = lax.rem(1 + 2 * t + t // 2, 4)
    dy = lax.rem(dx + 1 + lax.rem(index // 4, 4), 4)
    dc = 1 - index // 16
    return lax.rem(x + dx, 4), lax.rem(y + dy, 4), lax.rem(c + dc, 2)


def meet():
    x, z, y, c = place()
    barrier = pltpu.get_barrier_semaphore()

    @pl.loop(0, PLANE - 1)
    def _(index):
        px, py, pc = peer(index)
        pl.semaphore_signal(barrier, inc=1, device_id=device(px, z, py, pc), device_id_type=MESH)

    for step in (1, 7):
        pl.semaphore_signal(
            barrier, inc=1, device_id=device(x, lax.rem(z + step, 8), y, c), device_id_type=MESH
        )
    return barrier


def all_met(barrier):
    pl.semaphore_wait(barrier, PLANE + 1)


def remote(src, dst, send_sem, recv_sem, target):
    return pltpu.make_async_remote_copy(
        src_ref=src, dst_ref=dst, send_sem=send_sem, recv_sem=recv_sem, device_id=target, device_id_type=MESH
    )


def drain(ref, sem):
    pltpu.make_async_copy(ref, ref, sem).wait()


def adam(grad, weight, first, second):
    first = beta_one * first + (1.0 - beta_one) * grad
    second = beta_two * second + (1.0 - beta_two) * grad * grad
    step = learn_rate * (first / first_fix) / (jnp.sqrt(second / second_fix) + epsilon)
    return weight - step, first, second


def half_of(ring):
    return slice(12 * ring, 12 * ring + 12)


def kernel(
    count, prev, last, plan, hid_in, grd_in, weight_in, first_in, second_in, own, out,
    hid, grd, hid_t, part, pieces, acc, up_s, up_r, down_s, down_r, total, swap_s, swap_r,
    load_0, load_1, load_2, state, kept_grad, mine, back_s, back_r, whole,
    held_00, held_01, held_02, held_03, held_04, held_10, held_11, held_12, held_13, held_14,
    picked, result,
    load_sem, plane_send, plane_recv, self_sem, ring_send, ring_recv, swap_sem, back_sem,
    gather_send, gather_recv, spread_send, spread_recv, out_sem,
):
    held = ((held_00, held_01, held_02, held_03, held_04), (held_10, held_11, held_12, held_13, held_14))
    loads = (load_0, load_1, load_2)
    x, z, y, c = place()
    zplus, zminus = lax.rem(z + 1, 8), lax.rem(z + 7, 8)
    slot = (x * 4 + y) * 2 + c
    rows = hid.shape[0]
    copies = [pltpu.make_async_copy(hid_in, hid, load_sem.at[0]), pltpu.make_async_copy(grd_in, grd, load_sem.at[1])]
    for i, ref in enumerate((weight_in, first_in, second_in)):
        copies.append(pltpu.make_async_copy(ref, loads[i], load_sem.at[2 + i]))
    for copy in copies:
        copy.start()
    barrier = meet()
    live = lax.broadcasted_iota(jnp.int32, (256, 1), 0)
    copies[0].wait()

    for k in range(rows // 256):
        block = hid[k * 256 : (k + 1) * 256, :]
        kept = jnp.where(live + k * 256 < count[0, 0], block.astype(F32), 0.0)
        hid_t[:, k * 256 : (k + 1) * 256] = kept.T.astype(BF16)
    copies[1].wait()

    def multiply(half):
        for px in range(4):
            col = px * 512 + half * 128
            rhs = jnp.concatenate([grd[:, col : col + 128], grd[:, col + 256 : col + 384]], axis=1)
            out = jnp.dot(hid_t[...], rhs, preferred_element_type=F32)
            for dest in range(8):
                away = lax.rem(dest - z + 8, 8)
                pos = jnp.where(away == 0, 7, jnp.where(away < 4, 7 - 2 * away, 2 * (away - 4)))
                for py in range(4):
                    top = dest * 96 + py * 24
                    block = out[top : top + 24, :].astype(BF16)
                    part[pos, py, :, col : col + 128] = block[:, :128]
                    part[pos, py, :, col + 256 : col + 384] = block[:, 128:]

    def spread(half):
        for g, (a, b) in enumerate(OUT_GROUPS):

            @pl.loop(0, PLANE - 1)
            def _(index):
                px, py, pc = peer(index)
                col = pl.multiple_of(px * 512 + pc * 256 + half * 128, 128)
                remote(
                    part.at[a:b, py, :, pl.ds(col, 128)],
                    pieces.at[half, slot, a:b],
                    plane_send.at[half],
                    plane_recv.at[half, g],
                    device(px, z, py, pc),
                ).start()

        col = pl.multiple_of(x * 512 + c * 256 + half * 128, 128)
        pltpu.make_async_copy(
            part.at[:, y, :, pl.ds(col, 128)], pieces.at[half, slot], self_sem.at[half]
        ).start()

    def add_group(half, g):
        a, b = OUT_GROUPS[g]
        if g == 0:
            drain(pieces.at[half, 0], self_sem.at[half])
        drain(pieces.at[half, pl.ds(0, PLANE - 1), a:b], plane_recv.at[half, g])

        @pl.loop(0, PLANE)
        def _(i):
            acc[i, a:b] = pieces[half, i, a:b].astype(F32) + acc[prev[i], a:b]

        if g == 0:

            @pl.loop(0, EXPERTS // 2)
            def _(e):
                up_s[half, 0, e] = acc[last[e], 0].astype(BF16)
                down_s[half, 0, e] = acc[last[e + 12], 0].astype(BF16)

        else:
            for ring, (buf, r) in enumerate(((up_s, up_r), (down_s, down_r))):
                first = half_of(ring) if g == 1 else slice(0, EXPERTS)
                n = first.stop - first.start
                drain(r.at[half, g - 1, pl.ds(0, n)], ring_recv.at[half, ring, g - 1])
                pos = a + ring

                @pl.loop(0, n)
                def _(e):
                    buf[half, g, e + first.start] = (
                        acc[last[e + first.start], pos] + r[half, g - 1, e].astype(F32)
                    ).astype(BF16)

                if g == 1:

                    @pl.loop(0, EXPERTS - n)
                    def _(e):
                        other = e + (12 - first.start)
                        buf[half, g, other] = acc[last[other], pos].astype(BF16)

        n = 12 if g == 0 else EXPERTS
        for ring, (s, r, to) in enumerate(((up_s, up_r, zplus), (down_s, down_r, zminus))):
            remote(
                s.at[half, g, pl.ds(0, n)],
                r.at[half, g, pl.ds(0, n)],
                ring_send.at[half, ring, g],
                ring_recv.at[half, ring, g],
                device(x, to, y, c),
            ).start()

    def finish_sum(half):
        for ring, r in enumerate((up_r, down_r)):
            drain(r.at[half, 3], ring_recv.at[half, ring, 3])

        @pl.loop(0, EXPERTS)
        def _(e):
            total[half, e] = acc[last[e], 7] + up_r[half, 3, e].astype(F32) + down_r[half, 3, e].astype(F32)

        @pl.loop(0, EXPERTS)
        def _(e):
            low, high = total[half, e, 0:12, :], total[half, e, 12:24, :]
            kept_grad[half, e] = jnp.where(c == 0, low, high)
            swap_s[half, e] = jnp.where(c == 0, high, low)

        remote(
            swap_s.at[half], swap_r.at[half], swap_sem.at[half, 0], swap_sem.at[half, 1], device(x, z, y, 1 - c)
        ).start()

        @pl.loop(0, EXPERTS)
        def _(e):
            at = 2 * c + half
            mine[half, e] = adam(kept_grad[half, e], state[0, at, e], state[1, at, e], state[2, at, e])[0]

    def update(half):
        drain(swap_r.at[half], swap_sem.at[half, 1])

        @pl.loop(0, EXPERTS)
        def _(e):
            at = 2 * (1 - c) + half
            back_s[half, e] = adam(swap_r[half, e], state[0, at, e], state[1, at, e], state[2, at, e])[0]

        remote(
            back_s.at[half], back_r.at[half], back_sem.at[half, 0], back_sem.at[half, 1], device(x, z, y, 1 - c)
        ).start()

    def hop(half, k):
        for ring, to in enumerate((zplus, zminus)):
            src = 0 if k == 0 else ring
            dst = 0 if k == 3 else ring
            piece = pl.ds(12 * ring, 12) if k == 3 else pl.ds(0, EXPERTS)
            yield remote(
                held[half][k].at[src, piece],
                held[half][k + 1].at[dst, piece],
                gather_send.at[half, ring, k],
                gather_recv.at[half, ring, k],
                device(x, to, y, c),
            )

    def join(half):
        drain(back_r.at[half], back_sem.at[half, 1])

        @pl.loop(0, EXPERTS)
        def _(e):
            ours, theirs = mine[half, e], back_r[half, e]
            whole[half, e, 0:12, :] = jnp.where(c == 0, ours, theirs)
            whole[half, e, 12:24, :] = jnp.where(c == 0, theirs, ours)

        held[half][0][0] = whole[half].astype(BF16)
        for copy in hop(half, 0):
            copy.start()

    def place_group(half, g):
        a, b = IN_GROUPS[g]
        if g:
            for copy in hop(half, g - 1):
                copy.wait_recv()
            if g < 4:
                for copy in hop(half, g):
                    copy.start()
        col = pl.multiple_of(x * 512 + c * 256 + half * 128, 128)

        @pl.loop(0, PLANE - 1)
        def _(index):
            px, py, pc = peer(index)
            e = plan[px, z * 8 + py * 2 + pc]
            picked[half, index, a:b] = held[half][g][:, e]
            remote(
                picked.at[half, index, a:b],
                result.at[a:b, y, :, pl.ds(col, 128)],
                spread_send.at[half],
                spread_recv.at[g],
                device(px, z, py, pc),
            ).start()

        result[a:b, y, :, pl.ds(col, 128)] = held[half][g][:, plan[x, z * 8 + y * 2 + c]]

    multiply(0)
    all_met(barrier)
    spread(0)
    multiply(1)
    spread(1)
    acc[PLANE] = jnp.zeros_like(acc[PLANE])
    for i in range(3):
        copies[2 + i].wait()

        @pl.loop(0, 4)
        def _(at):
            for e in range(EXPERTS):
                state[i, at, e] = loads[i][:, e, pl.ds(pl.multiple_of(at * 128, 128), 128)]

    for g in range(4):
        add_group(0, g)
    finish_sum(0)
    add_group(1, 0)
    update(0)
    add_group(1, 1)
    join(0)
    add_group(1, 2)
    place_group(0, 0)
    add_group(1, 3)
    place_group(0, 1)
    finish_sum(1)
    place_group(0, 2)
    update(1)
    place_group(0, 3)
    join(1)
    place_group(0, 4)
    for g in range(5):
        place_group(1, g)

    @pl.loop(0, 2)
    def _(half):
        ours = pl.multiple_of(c * 256 + half * 128, 128)
        theirs = pl.multiple_of((1 - c) * 256 + half * 128, 128)
        for e in range(EXPERTS):
            own[:, e, pl.ds(ours, 128)] = kept_grad[half, e]
            own[:, e, pl.ds(theirs, 128)] = swap_r[half, e]

    for g, (a, b) in enumerate(IN_GROUPS):
        drain(picked.at[:, pl.ds(0, PLANE - 1), a:b], spread_recv.at[g])
        for pos in range(a, b):
            away = (0, 7, 1, 6, 2, 5, 3, 4)[pos]
            pltpu.make_async_copy(result.at[pos], out.at[lax.rem(z + away, 8)], out_sem.at[pos]).start()
    for pos in range(8):
        drain(result.at[pos], out_sem.at[pos])
    for half in range(2):
        drain(swap_s.at[half], swap_sem.at[half, 0])
        drain(back_s.at[half], back_sem.at[half, 0])
        drain(pieces.at[half, pl.ds(0, PLANE - 1)], plane_send.at[half])
        drain(picked.at[half, pl.ds(0, PLANE - 1)], spread_send.at[half])
        for g in range(4):
            n = 12 if g == 0 else EXPERTS
            for ring, s in enumerate((up_s, down_s)):
                drain(s.at[half, g, pl.ds(0, n)], ring_send.at[half, ring, g])
        for k in range(4):
            for copy in hop(half, k):
                copy.wait_send()


VMEM = pl.BlockSpec(memory_space=pltpu.VMEM)
SMEM = pl.BlockSpec(memory_space=pltpu.SMEM)
ANY = pl.BlockSpec(memory_space=pl.ANY)
DMA = pltpu.SemaphoreType.DMA


def run_kernel(*operands):
    block = (24, 24, 128)
    exchange = pltpu.VMEM((2, 24, 12, 128), F32)
    return pl.pallas_call(
        kernel,
        out_shape=(
            jax.ShapeDtypeStruct((12, 24, 512), F32),
            jax.ShapeDtypeStruct((8, 4, 24, 2048), BF16),
        ),
        in_specs=[SMEM] * 4 + [ANY] * 5,
        out_specs=(VMEM, ANY),
        scratch_shapes=[
            pltpu.VMEM((1024, 768), BF16),
            pltpu.VMEM((1024, 2048), BF16),
            pltpu.VMEM((768, 1024), BF16),
            pltpu.VMEM((8, 4, 24, 2048), BF16),
            pltpu.VMEM((2, 32, 8, 24, 128), BF16),
            pltpu.VMEM((33, 8, 24, 128), F32),
        ]
        + [pltpu.VMEM((2, 4) + block, BF16)] * 4
        + [pltpu.VMEM((2,) + block, F32), exchange, exchange]
        + [pltpu.VMEM((12, 24, 512), F32)] * 3
        + [pltpu.VMEM((3, 4, 24, 12, 128), F32)]
        + [exchange] * 4
        + [pltpu.VMEM((2,) + block, F32)]
        + [pltpu.VMEM((b - a,) + block, BF16) for _ in range(2) for a, b in IN_GROUPS]
        + [
            pltpu.VMEM((2, 31, 8, 24, 128), BF16),
            pltpu.VMEM((8, 4, 24, 2048), BF16),
            DMA((5,)),
            DMA((2,)),
            DMA((2, 4)),
            DMA((2,)),
            DMA((2, 2, 4)),
            DMA((2, 2, 4)),
            DMA((2, 2)),
            DMA((2, 2)),
            DMA((2, 2, 4)),
            DMA((2, 2, 4)),
            DMA((2,)),
            DMA((5,)),
            DMA((8,)),
        ],
        compiler_params=pltpu.CompilerParams(
            collective_id=0, has_side_effects=True, vmem_limit_bytes=56 * 2**20
        ),
        name="sum_and_place",
    )(*operands)


def per_device(hidden_acts, out_grads, row_counts, plan_now, plan_next, master, moment_one, moment_two):
    z = lax.axis_index("expert") // 8
    ids = lax.dynamic_slice_in_dim(plan_now, z * 8, 8, axis=1).reshape(PLANE)
    order = jnp.arange(PLANE, dtype=jnp.int32)
    earlier = (ids[None, :] == ids[:, None]) & (order[None, :] < order[:, None])
    prev = jnp.max(jnp.where(earlier, order[None, :], -1), axis=1)
    prev = jnp.where(prev < 0, PLANE, prev)
    named = ids[None, :] == jnp.arange(EXPERTS, dtype=jnp.int32)[:, None]
    last = jnp.max(jnp.where(named, order[None, :], -1), axis=1)
    last = jnp.where(last < 0, PLANE, last)
    states = [jnp.swapaxes(array, 0, 1) for array in (master, moment_one, moment_two)]
    grad_sum, replica = run_kernel(
        row_counts, prev, last, plan_next, hidden_acts[0, 0], out_grads[0, 0], *states
    )
    news = [jnp.swapaxes(array, 0, 1) for array in adam(grad_sum, *states)]
    return (*news, replica.reshape(1, 1, 768, 2048))


def solution(mesh):
    state = P(None, "expert", "dp")
    split = P("dp", "expert", None, None)
    return jax.shard_map(
        per_device,
        mesh=mesh,
        in_specs=(split, split, P("dp", "expert"), P(), P(), state, state, state),
        out_specs=(state, state, state, split),
        check_vma=False,
    )
```

time: 130 us -> 112 us (0.86)
  Pallas kernels: 117 us -> 104 us
  local copies, waits for them, and re-layouts: 7.64 us -> 1.85 us
    pallas_call x2 -> x1, Pallas kernels: 117 us -> 104 us  [run_kernel(): pl.pallas_call(kernel, out_shape=(jax.ShapeDtypeStruct((12, 24, 512), F32...]
    unnamed x14 -> x11, local copies, waits for them, and re-layouts: 7.48 us -> 1.7 us
    transpose x0 -> x1, other arithmetic: none -> 2.8 us  [per_device(): news = [jnp.swapaxes(array, 0, 1) for array in adam(grad_sum, *states)]]
    sub x1 -> x0, other arithmetic: 2.54 us -> none  [per_device(): master - learn_rate * (moment_one_new / first_fix) / (jnp.sqrt(moment_two...]
where the time goes in v2:
time: 112 us
  Pallas kernels  104 us (93%)
  other arithmetic  4.13 us (4%)
  local copies, waits for them, and re-layouts  1.85 us (2%)
  between operations  1.35 us (1%)
    pallas_call x1, Pallas kernels, run_kernel(): pl.pallas_call(kernel, out_shape=(jax.ShapeDtypeStruct((12, 24, 512), F32...  104 us
    transpose x1, other arithmetic, per_device(): news = [jnp.swapaxes(array, 0, 1) for array in adam(grad_sum, *states)]  2.8 us

profile of v2, /device:TPU:1, one launch (start us, length us, event | category | flops | bytes accessed | tf_op | source)
XLA Modules:
  0.0 111.8 jit_solution(16635832601673544329)
XLA Ops:
  0.6 0.0 copy-start
  1.3 0.0 copy-done
  1.3 0.1 constant_dynamic-slice_fusion
  1.4 0.1 eq.28
  1.5 0.1 select_reduce_fusion.1
  1.6 0.2 select_reduce_fusion
  1.8 0.5 compare_select_fusion.1.prev
  2.3 0.5 compare_select_fusion.last
  2.8 0.0 copy-start.2
  2.8 0.0 copy-start.3
  2.8 0.0 copy-start.4
  2.8 104.4 %sum_and_place.1 = (f32[12,24,512]{2,1,0:T(8,128)}, bf16[8,4,24,2048]{3,2,1,0:T(8,128)(2,1)}) custom-call(s32[1,1]{1,0:T(1,128)S(6)} %copy.13.count, s32[32]{0:T(128)} %compare_select_fusion.1.prev, s32[24]{0:T(128)} %compare_select_fusion.last, s32[4,64]{1,0:T(4,128)} %plan.1, bf16[1024,768]{1,0:T(8,128)(2,1)} %bitcast.22, bf16[1024,2048]{1,0:T(8,128)(2,1)} %bitcast.17, ...), custom_call_target="tpu_custom_call" | custom-call | tf_op jit(solution)/shard_map/sum_and_place/pallas_call | solution.py:354
  107.2 0.0 copy-start.1
  107.3 0.0 copy-done.2
  107.3 0.0 copy-done.3
  107.3 0.0 copy-done.4
  107.3 2.8 %fusion.2 = (f32[24,12,512]{2,0,1:T(8,128)}, f32[24,12,512]{2,0,1:T(8,128)}, f32[24,12,512]{2,0,1:T(8,128)}) fusion(f32[12,24,512]{2,1,0:T(8,128)} %get-tuple-element.6, f32[24,12,512]{2,0,1:T(8,128)S(1)} %copy-done.4, f32[24,12,512]{2,0,1:T(8,128)S(1)} %copy-done.3, f32[24,12,512]{2,0,1:T(8,128)S(1)} %copy-done.2), kind=kLoop, calls=%fused_computation.5 | loop fusion | flops 1769472 | bytes 4128768 | tf_op jit(solution)/shard_map/transpose | solution.py:415
  110.1 0.0 copy-done.1
  110.1 1.7 %copy.14 = bf16[1,1,768,2048]{3,2,1,0:T(8,128)(2,1)} copy(bf16[1,1,768,2048]{3,2,1,0:T(8,128)(2,1)S(1)} %bitcast.18) | data formatting | bytes 6291456
Async XLA Ops:
  0.6 0.7 copy-start
  2.8 104.4 %copy-start.2 = (f32[24,12,512]{2,0,1:T(8,128)S(1)}, f32[24,12,512]{2,0,1:T(8,128)}, u32[]{:S(2)}) copy-start(f32[24,12,512]{2,0,1:T(8,128)} %param.13) | copy-start | bytes 1769476
  2.8 104.4 %copy-start.3 = (f32[24,12,512]{2,0,1:T(8,128)S(1)}, f32[24,12,512]{2,0,1:T(8,128)}, u32[]{:S(2)}) copy-start(f32[24,12,512]{2,0,1:T(8,128)} %param.14) | copy-start | bytes 1769476
  2.8 104.5 %copy-start.4 = (f32[24,12,512]{2,0,1:T(8,128)S(1)}, f32[24,12,512]{2,0,1:T(8,128)}, u32[]{:S(2)}) copy-start(f32[24,12,512]{2,0,1:T(8,128)} %param.15) | copy-start | bytes 1769476
  107.2 2.8 %copy-start.1 = (bf16[8,4,24,2048]{3,2,1,0:T(8,128)(2,1)S(1)}, bf16[8,4,24,2048]{3,2,1,0:T(8,128)(2,1)}, u32[]{:S(2)}) copy-start(bf16[8,4,24,2048]{3,2,1,0:T(8,128)(2,1)} %get-tuple-element.7) | copy-start | bytes 9437188

commit v3 on v2

--- a/solution.py
+++ b/solution.py
@@ -32,23 +32,37 @@
     return (x, z * 8 + y * 2 + c)
 
 
-def peer(index):
+def wrap(value, size):
+    return jnp.where(value >= size, value - size, value)
+
+
+def each_peer(body):
     x, z, y, c = place()
-    t = lax.rem(index, 4)
-    dx = lax.rem(1 + 2 * t + t // 2, 4)
-    dy = lax.rem(dx + 1 + lax.rem(index // 4, 4), 4)
-    dc = 1 - index // 16
-    return lax.rem(x + dx, 4), lax.rem(y + dy, 4), lax.rem(c + dc, 2)
+    near = [wrap(x + dx, 4) for dx in range(4)]
+
+    def four(j, count):
+        far = jnp.where(j >= 4, j - 4, j)
+        core = jnp.where(j >= 4, c, 1 - c)
+        across = wrap(y + far, 4)
+        for t in range(count):
+            dx = (1 + 2 * t + t // 2) % 4
+            body(4 * j + t, near[dx], wrap(across + (dx + 1) % 4, 4), core)
+
+    @pl.loop(0, 7)
+    def _(j):
+        four(j, 4)
+
+    four(jnp.int32(7), 3)
 
 
 def meet():
     x, z, y, c = place()
     barrier = pltpu.get_barrier_semaphore()
 
-    @pl.loop(0, PLANE - 1)
-    def _(index):
-        px, py, pc = peer(index)
+    def greet(index, px, py, pc):
         pl.semaphore_signal(barrier, inc=1, device_id=device(px, z, py, pc), device_id_type=MESH)
+
+    each_peer(greet)
 
     for step in (1, 7):
         pl.semaphore_signal(
@@ -129,9 +143,7 @@
     def spread(half):
         for g, (a, b) in enumerate(OUT_GROUPS):
 
-            @pl.loop(0, PLANE - 1)
-            def _(index):
-                px, py, pc = peer(index)
+            def send(index, px, py, pc):
                 col = pl.multiple_of(px * 512 + pc * 256 + half * 128, 128)
                 remote(
                     part.at[a:b, py, :, pl.ds(col, 128)],
@@ -140,6 +152,8 @@
                     plane_recv.at[half, g],
                     device(px, z, py, pc),
                 ).start()
+
+            each_peer(send)
 
         col = pl.multiple_of(x * 512 + c * 256 + half * 128, 128)
         pltpu.make_async_copy(
@@ -264,9 +278,7 @@
                     copy.start()
         col = pl.multiple_of(x * 512 + c * 256 + half * 128, 128)
 
-        @pl.loop(0, PLANE - 1)
-        def _(index):
-            px, py, pc = peer(index)
+        def send(index, px, py, pc):
             e = plan[px, z * 8 + py * 2 + pc]
             picked[half, index, a:b] = held[half][g][:, e]
             remote(
@@ -277,6 +289,7 @@
                 device(px, z, py, pc),
             ).start()
 
+        each_peer(send)
         result[a:b, y, :, pl.ds(col, 128)] = held[half][g][:, plan[x, z * 8 + y * 2 + c]]
 
     multiply(0)

time: 112 us -> 105 us (0.938)
  Pallas kernels: 104 us -> 97.7 us
    pallas_call x1, Pallas kernels: 104 us -> 97.7 us  [run_kernel(): pl.pallas_call(kernel, out_shape=(jax.ShapeDtypeStruct((12, 24, 512), F32...]
where the time goes in v3:
time: 105 us
  Pallas kernels  97.7 us (93%)
  other arithmetic  4.13 us (4%)
  local copies, waits for them, and re-layouts  1.85 us (2%)
  between operations  1.35 us (1%)
    pallas_call x1, Pallas kernels, run_kernel(): pl.pallas_call(kernel, out_shape=(jax.ShapeDtypeStruct((12, 24, 512), F32...  97.7 us
    transpose x1, other arithmetic, per_device(): news = [jnp.swapaxes(array, 0, 1) for array in adam(grad_sum, *states)]  2.8 us

profile of v3, /device:TPU:1, one launch (start us, length us, event | category | flops | bytes accessed | tf_op | source)
XLA Modules:
  0.0 105.1 jit_solution(13131185698138303281)
XLA Ops:
  0.6 0.0 copy-start
  1.3 0.0 copy-done
  1.3 0.1 constant_dynamic-slice_fusion
  1.4 0.1 eq.28
  1.5 0.1 select_reduce_fusion.1
  1.6 0.2 select_reduce_fusion
  1.8 0.5 compare_select_fusion.1.prev
  2.3 0.5 compare_select_fusion.last
  2.8 0.0 copy-start.2
  2.8 0.0 copy-start.3
  2.8 0.0 copy-start.4
  2.8 97.7 %sum_and_place.1 = (f32[12,24,512]{2,1,0:T(8,128)}, bf16[8,4,24,2048]{3,2,1,0:T(8,128)(2,1)}) custom-call(s32[1,1]{1,0:T(1,128)S(6)} %copy.13.count, s32[32]{0:T(128)} %compare_select_fusion.1.prev, s32[24]{0:T(128)} %compare_select_fusion.last, s32[4,64]{1,0:T(4,128)} %plan.1, bf16[1024,768]{1,0:T(8,128)(2,1)} %bitcast.22, bf16[1024,2048]{1,0:T(8,128)(2,1)} %bitcast.17, ...), custom_call_target="tpu_custom_call" | custom-call | tf_op jit(solution)/shard_map/sum_and_place/pallas_call | solution.py:367
  100.6 0.0 copy-start.1
  100.6 0.0 copy-done.2
  100.6 0.0 copy-done.3
  100.6 0.0 copy-done.4
  100.6 2.8 %fusion.2 = (f32[24,12,512]{2,0,1:T(8,128)}, f32[24,12,512]{2,0,1:T(8,128)}, f32[24,12,512]{2,0,1:T(8,128)}) fusion(f32[12,24,512]{2,1,0:T(8,128)} %get-tuple-element.6, f32[24,12,512]{2,0,1:T(8,128)S(1)} %copy-done.4, f32[24,12,512]{2,0,1:T(8,128)S(1)} %copy-done.3, f32[24,12,512]{2,0,1:T(8,128)S(1)} %copy-done.2), kind=kLoop, calls=%fused_computation.5 | loop fusion | flops 1769472 | bytes 4128768 | tf_op jit(solution)/shard_map/transpose | solution.py:428
  103.4 0.0 copy-done.1
  103.4 1.7 %copy.14 = bf16[1,1,768,2048]{3,2,1,0:T(8,128)(2,1)} copy(bf16[1,1,768,2048]{3,2,1,0:T(8,128)(2,1)S(1)} %bitcast.18) | data formatting | bytes 6291456
Async XLA Ops:
  0.6 0.7 copy-start
  2.8 97.8 %copy-start.2 = (f32[24,12,512]{2,0,1:T(8,128)S(1)}, f32[24,12,512]{2,0,1:T(8,128)}, u32[]{:S(2)}) copy-start(f32[24,12,512]{2,0,1:T(8,128)} %param.13) | copy-start | bytes 1769476
  2.8 97.8 %copy-start.3 = (f32[24,12,512]{2,0,1:T(8,128)S(1)}, f32[24,12,512]{2,0,1:T(8,128)}, u32[]{:S(2)}) copy-start(f32[24,12,512]{2,0,1:T(8,128)} %param.14) | copy-start | bytes 1769476
  2.8 97.8 %copy-start.4 = (f32[24,12,512]{2,0,1:T(8,128)S(1)}, f32[24,12,512]{2,0,1:T(8,128)}, u32[]{:S(2)}) copy-start(f32[24,12,512]{2,0,1:T(8,128)} %param.15) | copy-start | bytes 1769476
  100.6 2.8 %copy-start.1 = (bf16[8,4,24,2048]{3,2,1,0:T(8,128)(2,1)S(1)}, bf16[8,4,24,2048]{3,2,1,0:T(8,128)(2,1)}, u32[]{:S(2)}) copy-start(bf16[8,4,24,2048]{3,2,1,0:T(8,128)(2,1)} %get-tuple-element.7) | copy-start | bytes 9437188
